TPU v7x, 32 devices: a whole 2x2x4 slice. The times are simulated.
32 devices in a mesh: aux: 8 (over y, x, core), shell: 4 (over z).
Axes of the slice: x: 2, y: 2, z: 4, core: 2. Of those that a mesh axis runs over, the one named last changes fastest.
Arguments:
- density: bfloat16 [32, 120, 8192], P('aux', None, 'shell'), may hold values from -6 to 6
- occ_density: bfloat16 [32, 120, 120], P('aux'), may hold values from -6 to 6
- cabs_coeff: bfloat16 [2048, 8192], P('aux', 'shell'), may hold values from -0.0625 to 0.0625
- occ_coeff: bfloat16 [2048, 120], P('aux'), may hold values from -0.5 to 0.5
- tile_owner: int32 [16, 1], replicated, may hold values from 0 to 3; in each aligned block of 16 rows (0 to 15, 16 to 31, ...) at most 8 rows name the same one
Outputs:
- ao_density: bfloat16 [32, 32, 128, 2048], P('shell', 'aux')
Inputs may be any that keep to these rules, and one draw needn't show every extreme that they name: `tile_owner`: no owner holds more than 8 blocks, and some owner holds exactly 8; every owner holds at least one block.
All inputs are finite; a program needn't handle non-finite values.
Results may differ from a plain program's by a relative error of at most 0.015.
Values may be sent and summed in bfloat16 or wider, within the bound.
No kernel may reach another device: no remote copies, remote signals or barrier semaphores. Data moves between devices by JAX's collectives and lax.ppermute only.
A program may use at most 64 MiB of HBM per device.

v0:
```python
import jax
import jax.numpy as jnp
from jax import lax
from jax.sharding import PartitionSpec as P

NOCC = 120
CAPT = 8


def per_device(density, occ_density, cabs_coeff, occ_coeff, tile_owner):
    local_q = density.shape[0]
    owners = lax.axis_size("shell")
    me_shell = lax.axis_index("shell")
    occ_full = lax.all_gather(occ_coeff, "aux", axis=0, tiled=True)
    nao = occ_full.shape[0]
    ntile = tile_owner.shape[0]
    width = nao // ntile
    share_cols = nao // owners
    owned = (tile_owner[:, 0] == me_shell).astype(jnp.int32)
    rank = jnp.cumsum(owned) - 1
    select = (
        (rank[None, :] == jnp.arange(CAPT, dtype=jnp.int32)[:, None]) & (owned[None, :] == 1)
    ).astype(jnp.bfloat16)
    batches = 2
    span = local_q // batches
    results = []
    for batch in range(batches):
        dens = density[batch * span : (batch + 1) * span]
        occ_dens = occ_density[batch * span : (batch + 1) * span]
        flat = dens.reshape(span * NOCC, dens.shape[2])
        terms = lax.dot_general(
            flat,
            lax.all_gather(cabs_coeff, "aux", axis=0, tiled=True),
            (((1,), (1,)), ((), ())),
            preferred_element_type=jnp.float32,
        )
        mine = lax.psum_scatter(
            terms.astype(jnp.bfloat16), "shell", scatter_dimension=1, tiled=True
        ).astype(jnp.float32)
        my_rows = lax.dynamic_slice_in_dim(occ_full, me_shell * share_cols, share_cols, 0)
        occ_term = jnp.einsum("qij,nj->qin", occ_dens, my_rows, preferred_element_type=jnp.float32)
        rounded = (mine + occ_term.reshape(span * NOCC, share_cols)).astype(jnp.bfloat16)
        spread = lax.all_gather(rounded, "shell", axis=1, tiled=True)
        blocks = spread.reshape(span, NOCC, ntile, width)
        half_owned = jnp.einsum(
            "kt,qitw->kqiw", select, blocks, preferred_element_type=jnp.float32
        ).astype(jnp.bfloat16)
        gamma = jnp.einsum(
            "kqiw,mi->kqwm", half_owned, occ_full, preferred_element_type=jnp.float32
        )
        results.append(gamma.astype(jnp.bfloat16))
    return jnp.concatenate(results, axis=1)


def solution(mesh):
    in_specs = (
        P("aux", None, "shell"),
        P("aux", None, None),
        P("aux", "shell"),
        P("aux", None),
        P(),
    )
    out_specs = P("shell", "aux", None, None)
    return jax.shard_map(
        per_device, mesh=mesh, in_specs=in_specs, out_specs=out_specs, check_vma=False
    )
```

profile of v0, /device:TPU:0, one launch (start us, length us, event | category | flops | bytes accessed | tf_op | source)
XLA Modules:
  0.0 177.0 jit_solution(4344469540848584070)
XLA Ops:
  6.5 0.0 all-gather.2.cloned.1.call-start
  6.5 0.7 all-gather.2.cloned.1.call-update
  7.3 0.0 reduce-scatter.3.cloned.1.call-start
  7.3 1.6 fusion.26
  8.9 57.3 %all-gather.2.cloned.1.call-done = bf16[2048,2048]{1,0:T(8,128)(2,1)} async-done(((bf16[256,2048]{1,0:T(8,128)(2,1)}), bf16[2048,2048]{1,0:T(8,128)(2,1)}) %all-gather.2.cloned.1.call-update) | async-done | bytes 8388624 | tf_op jit(solution)/shard_map/all_gather | solution.py:33
  66.2 6.8 %convolution_convert_fusion.3 = bf16[240,2048]{1,0:T(8,128)(2,1)} fusion(bf16[240,2048]{1,0:T(8,128)(2,1)S(1)} %bitcast.57, bf16[2048,2048]{1,0:T(8,128)(2,1)} %all-gather.2.cloned.1.call-done), kind=kOutput, calls=%fused_computation.4 | convolution fusion | flops 2013757440 | bytes 10354688 | tf_op jit(solution)/shard_map/dot_general | solution.py:31
  73.0 0.0 copy-start.2
  73.0 0.0 reduce-scatter.3.cloned.1.call-update
  73.0 0.0 reduce-scatter.5.cloned.1.call-start
  73.1 6.7 %convolution_convert_fusion.2 = bf16[240,2048]{1,0:T(8,128)(2,1)} fusion(bf16[240,2048]{1,0:T(8,128)(2,1)S(1)} %bitcast.56, bf16[2048,2048]{1,0:T(8,128)(2,1)} %all-gather.2.cloned.1.call-done), kind=kOutput, calls=%fused_computation.3 | convolution fusion | flops 2013757440 | bytes 10354688 | tf_op jit(solution)/shard_map/dot_general | solution.py:31
  79.8 0.0 reduce-scatter.5.cloned.1.call-update
  79.8 0.0 copy-done.2
  79.9 0.1 copy.7
  80.0 0.0 copy-done.1
  80.0 10.9 %all_gather.14 = bf16[2048,120]{0,1:T(8,128)(2,1)S(1)} all-gather(bf16[256,120]{0,1:T(8,128)(2,1)S(1)} %copy-done.1), channel_id=1, replica_groups=mesh['aux'=8,'shell'=4] {'aux'}, dimensions={0}, use_global_device_ids=true | all-gather | bytes 552960 | tf_op jit(solution)/shard_map/all_gather | solution.py:14
  90.8 0.1 add_reduce_fusion
  91.0 0.0 copy-done
  91.0 0.2 fusion.8
  91.2 0.2 fusion.10
  91.4 8.0 %reduce-scatter.3.cloned.1.call-done = bf16[240,512]{1,0:T(8,128)(2,1)} async-done(((bf16[240,2048]{1,0:T(8,128)(2,1)}), bf16[240,512]{1,0:T(8,128)(2,1)}) %reduce-scatter.3.cloned.1.call-update) | async-done | bytes 245776 | tf_op jit(solution)/shard_map/reduce_scatter | solution.py:37
  99.5 1.0 fusion.5
  100.5 31.1 %all_gather.15 = bf16[240,2048]{1,0:T(8,128)(2,1)S(1)} all-gather(bf16[240,512]{1,0:T(8,128)(2,1)S(1)} %fusion.5), channel_id=1, replica_groups=mesh['aux'=8,'shell'=4] {'shell'}, dimensions={1}, use_global_device_ids=true | all-gather | bytes 1228800 | tf_op jit(solution)/shard_map/all_gather | solution.py:43
  131.5 0.2 copy.12
  131.8 4.9 %reduce-scatter.5.cloned.1.call-done = bf16[240,512]{1,0:T(8,128)(2,1)} async-done(((bf16[240,2048]{1,0:T(8,128)(2,1)}), bf16[240,512]{1,0:T(8,128)(2,1)}) %reduce-scatter.5.cloned.1.call-update) | async-done | bytes 245776 | tf_op jit(solution)/shard_map/reduce_scatter | solution.py:37
  136.7 1.0 fusion.4
  137.7 20.5 %all_gather.16 = bf16[240,2048]{1,0:T(8,128)(2,1)S(1)} all-gather(bf16[240,512]{1,0:T(8,128)(2,1)S(1)} %fusion.4), channel_id=1, replica_groups=mesh['aux'=8,'shell'=4] {'shell'}, dimensions={1}, use_global_device_ids=true | all-gather | bytes 1228800 | tf_op jit(solution)/shard_map/all_gather | solution.py:43
  158.2 0.2 copy.13
  158.4 0.3 fusion.2
  158.7 0.3 fusion
  159.0 2.4 %convolution_convert_fusion = bf16[8,2,128,2048]{3,2,1,0:T(8,128)(2,1)S(1)} fusion(bf16[8,2,120,128]{3,0,2,1:T(8,128)(2,1)S(1)} %fusion, bf16[2048,120]{0,1:T(8,128)(2,1)S(1)} %all_gather.14), kind=kOutput, calls=%fused_computation.1 | convolution fusion | flops 1010827264 | bytes 9371648 | tf_op jit(solution)/shard_map/kqiw,mi->kqwm/dot_general | solution.py:48
  161.4 2.4 %convolution_convert_fusion.1 = bf16[8,2,128,2048]{3,2,1,0:T(8,128)(2,1)S(1)} fusion(bf16[8,2,120,128]{3,0,2,1:T(8,128)(2,1)S(1)} %fusion.2, bf16[2048,120]{0,1:T(8,128)(2,1)S(1)} %all_gather.14), kind=kOutput, calls=%fused_computation.2 | convolution fusion | flops 1010827264 | bytes 9371648 | tf_op jit(solution)/shard_map/kqiw,mi->kqwm/dot_general | solution.py:48
  163.8 6.7 %pad_maximum_fusion = bf16[8,4,128,2048]{3,2,1,0:T(8,128)(2,1)} fusion(bf16[8,2,128,2048]{3,2,1,0:T(8,128)(2,1)S(1)} %convolution_convert_fusion, bf16[8,2,128,2048]{3,2,1,0:T(8,128)(2,1)S(1)} %convolution_convert_fusion.1), kind=kLoop, calls=%fused_computation | loop fusion | flops 8388608 | bytes 33554432 | tf_op jit(solution)/shard_map/concatenate | solution.py:52
  (4 shorter events, 0.0 us)
Async XLA Ops:
  6.5 59.7 %all-gather.2.cloned.1.call-start = ((), (), s32[]{:S(2)}) async-start(), calls=%async_computation.2 | async-start | bytes 9437184 | tf_op jit(solution)/shard_map/all_gather | solution.py:33
  7.3 92.2 %reduce-scatter.3.cloned.1.call-start = ((), (), s32[]{:S(2)}) async-start(), calls=%async_computation.3 | async-start | bytes 1228800 | tf_op jit(solution)/shard_map/reduce_scatter | solution.py:37
  73.0 6.8 %copy-start.2 = (s32[16,1]{0,1:T(1,128)S(1)}, s32[16,1]{0,1:T(1,128)}, u32[]{:S(2)}) copy-start(s32[16,1]{0,1:T(1,128)} %param.9) | copy-start | bytes 196
  73.0 7.0 %copy-start.1 = (bf16[256,120]{0,1:T(8,128)(2,1)S(1)}, bf16[256,120]{0,1:T(8,128)(2,1)}, u32[]{:S(2)}) copy-start(bf16[256,120]{0,1:T(8,128)(2,1)} %param.8) | copy-start | bytes 184324
  73.0 17.9 %copy-start = (bf16[4,120,120]{2,1,0:T(8,128)(2,1)S(1)}, bf16[4,120,120]{2,1,0:T(8,128)(2,1)}, u32[]{:S(2)}) copy-start(bf16[4,120,120]{2,1,0:T(8,128)(2,1)} %param.6) | copy-start | bytes 345604
  73.0 63.6 %reduce-scatter.5.cloned.1.call-start = ((), (), s32[]{:S(2)}) async-start(), calls=%async_computation.4 | async-start | bytes 1228800 | tf_op jit(solution)/shard_map/reduce_scatter | solution.py:37
Sparse Core Ops, SparseCore 0:
  9.2 56.9 all-gather.1
  73.2 26.2 reduce-scatter.2
  101.8 34.8 reduce-scatter.4
where the time goes:
time: 177 us
  waiting for transfers between devices  71 us (40%)
  blocking collectives  62.4 us (35%)
  matrix products  19.3 us (11%)
  between operations  13.2 us (7%)
  other arithmetic  8.89 us (5%)
  local copies, waits for them, and re-layouts  2.12 us (1%)
    all_gather x1, waiting for transfers between devices, per_device(): lax.all_gather(cabs_coeff, 'aux', axis=0, tiled=True)  57.3 us
    all_gather x2, blocking collectives, per_device(): spread = lax.all_gather(rounded, 'shell', axis=1, tiled=True)  51.6 us
    dot_general x2, matrix products, per_device(): lax.dot_general(flat, lax.all_gather(cabs_coeff, 'aux', axis=0, tiled=Tru...  13.5 us
    reduce_scatter x2, waiting for transfers between devices, per_device(): lax.psum_scatter(terms.astype(jnp.bfloat16), 'shell', scatter_dimension=1...  12.9 us
    all_gather x1, blocking collectives, per_device(): occ_full = lax.all_gather(occ_coeff, 'aux', axis=0, tiled=True)  10.9 us
    concatenate x1, other arithmetic, per_device(): return jnp.concatenate(results, axis=1)  6.71 us
    dot_general x2, matrix products, per_device(): jnp.einsum('kqiw,mi->kqwm', half_owned, occ_full, preferred_element_type=...  4.81 us
  transfers between devices with their start and end apart: 3, of which 3 were waited for; matrix products, arithmetic and copies ran while one was open for 6% of the time, Pallas kernels for 0%

commit v1 on v0

v1 whole, which is shorter than its diff:
```python
import functools
import math

import jax
import jax.numpy as jnp
from jax import lax
from jax.experimental import pallas as pl
from jax.experimental.pallas import tpu as pltpu
from jax.sharding import PartitionSpec as P

CAPT = 8
LANES = 128
CORES = 2
GRANT = 12 * 1024 * 1024
VMEM = pl.BlockSpec(memory_space=pltpu.VMEM)
ANY = pl.BlockSpec(memory_space=pl.ANY)
SMEM = pl.BlockSpec(memory_space=pltpu.SMEM)


def call(kernel, out_shape, in_specs, out_specs, flops, size, scratch=(), aliases=None):
    return pl.pallas_call(
        kernel,
        out_shape=out_shape,
        in_specs=in_specs,
        out_specs=out_specs,
        scratch_shapes=list(scratch),
        input_output_aliases=aliases or {},
        compiler_params=pltpu.CompilerParams(vmem_limit_bytes=GRANT),
        cost_estimate=pl.CostEstimate(flops=flops, bytes_accessed=size, transcendentals=0),
    )


def matmul_kernel(left_ref, occ_ref, first_ref, second_ref, out_ref):
    depth, nocc = left_ref.shape[1], occ_ref.shape[1]
    rows = first_ref.shape[0]
    dims = (((1,), (1,)), ((), ()))
    for k, right_ref in enumerate((first_ref, second_ref)):
        cols = slice(k * rows, (k + 1) * rows)

        def product():
            return lax.dot_general(
                left_ref[...], right_ref[:, :depth], dims, preferred_element_type=jnp.float32
            )

        @pl.when(lax.axis_index("shell") == 0)
        def _():
            occ = lax.dot_general(
                occ_ref[...],
                right_ref[:, depth : depth + nocc],
                dims,
                preferred_element_type=jnp.float32,
            )
            out_ref[:, cols] = (product() + occ).astype(out_ref.dtype)

        @pl.when(lax.axis_index("shell") != 0)
        def _():
            out_ref[:, cols] = product().astype(out_ref.dtype)


def matmul(left, occ, first, second):
    rows, depth = left.shape
    cols = 2 * first.shape[0]
    return call(
        matmul_kernel,
        jax.ShapeDtypeStruct((rows, cols), left.dtype),
        [VMEM] * 4,
        VMEM,
        2 * rows * depth * cols,
        2 * (rows + cols) * depth,
    )(left, occ, first, second)


def send_kernel(owners, groups, *refs):
    me = lax.axis_index("shell")
    outs = refs[-len(groups) :]
    at = 0
    for out_ref, hops in zip(outs, groups):
        for hop in hops:
            part_ref = refs[at]
            before_ref = refs[at + 1] if hop else None
            at += 2 if hop else 1

            def write(part_ref=part_ref, before_ref=before_ref, out_ref=out_ref):
                if before_ref is None:
                    out_ref[...] = part_ref[...]
                else:
                    out_ref[...] = part_ref[...] + before_ref[...]

            pl.when((me == hop) | (me == owners - 1 - hop))(write)


def send(owners, groups, values):
    flat = [v for hops in values for pair in hops for v in pair]
    shape = jax.ShapeDtypeStruct(flat[0].shape, flat[0].dtype)
    size = 2 * math.prod(shape.shape)
    return call(
        functools.partial(send_kernel, owners, groups),
        [shape] * len(groups),
        [VMEM] * len(flat),
        [VMEM] * len(groups),
        size * len(groups),
        3 * size * len(groups),
    )(*flat)


def zero_kernel(owner_ref, out_ref, zero, sem):
    me = lax.axis_index("shell")
    count = jnp.int32(0)
    for tile in range(owner_ref.shape[0]):
        count += jnp.where(owner_ref[tile] == me, 1, 0)
    zero[...] = jnp.zeros_like(zero)
    for wait in (False, True):
        for slot in range(out_ref.shape[0]):

            @pl.when(slot >= count)
            def _():
                for q in range(out_ref.shape[1]):
                    copy = pltpu.make_async_copy(zero, out_ref.at[slot, q], sem.at[slot, q])
                    copy.wait() if wait else copy.start()


def zero_slots(owner, shape, dtype):
    return call(
        zero_kernel,
        jax.ShapeDtypeStruct(shape, dtype),
        [SMEM],
        ANY,
        0,
        math.prod(shape),
        [pltpu.VMEM(shape[2:], dtype), pltpu.SemaphoreType.DMA(shape[:2])],
    )(owner)


def occ_kernel(number, depth, table_ref, first_ref, second_ref, *refs):
    out_ref, sem = refs[-2:]
    me = lax.axis_index("aux")
    rows = first_ref.shape[0]
    copies = []
    for k, piece in enumerate((first_ref, second_ref)):
        start = pl.multiple_of(table_ref[number, me ^ k] * rows, 8)
        copies.append(
            pltpu.make_async_copy(
                piece.at[:, pl.ds(depth, LANES)], out_ref.at[pl.ds(start, rows)], sem.at[k]
            )
        )
    for copy in copies:
        copy.start()
    for copy in copies:
        copy.wait()


def put_occ(table, number, first, second, nao, depth, before):
    rows = first.shape[0]
    old = [] if before is None else [before]
    return call(
        functools.partial(occ_kernel, number, depth),
        jax.ShapeDtypeStruct((nao, LANES), first.dtype),
        [SMEM] + [ANY] * (2 + len(old)),
        ANY,
        0,
        8 * rows * LANES,
        [pltpu.SemaphoreType.DMA((2,))],
        {3: 0} if old else None,
    )(table, first, second, *old)


def final_kernel(nocc, chunk, near_of, owner_ref, table_ref, *refs):
    parts, occ_ref, out_ref, stage, sem = refs[: len(near_of)], *refs[-5:-4], *refs[-3:]
    me, here = lax.axis_index("aux"), lax.axis_index("shell")
    span, width = out_ref.shape[1], out_ref.shape[2]
    tiles = parts[0].shape[1] // width
    ntile = owner_ref.shape[0]
    for t in range(tiles):
        source = table_ref[chunk, me ^ (t * 2 // tiles)]
        tile = source * (tiles // 2) + t % (tiles // 2)
        slot = jnp.int32(0)
        for other in range(ntile):
            slot += jnp.where((owner_ref[other] == here) & (other < tile), 1, 0)

        @pl.when(owner_ref[tile] == here)
        def _(t=t, slot=slot):
            copies = []
            for q in range(span):
                rows, cols = pl.ds(q * nocc, nocc), pl.ds(t * width, width)
                half = jnp.zeros((nocc, width), jnp.float32)
                for part, hops in zip(parts, near_of):
                    value = part[rows, cols].astype(jnp.float32)
                    if hops is not None:
                        near = functools.reduce(
                            jnp.logical_or, [(here == h) for h in hops]
                        )
                        value = jnp.where(near, value, 0.0)
                    half = half + value
                half = half.astype(out_ref.dtype)
                stage[q] = lax.dot_general(
                    half,
                    occ_ref[:, pl.ds(0, nocc)],
                    (((0,), (1,)), ((), ())),
                    preferred_element_type=jnp.float32,
                ).astype(out_ref.dtype)
                copy = pltpu.make_async_copy(stage.at[q], out_ref.at[slot, q], sem.at[q])
                copy.start()
                copies.append(copy)
            for copy in copies:
                copy.wait()


def final(owner, table, chunk, parts, near_of, occ_full, out, nocc):
    _, span, width, nao = out.shape
    tiles = parts[0].shape[1] // width
    return call(
        functools.partial(final_kernel, nocc, chunk, near_of),
        jax.ShapeDtypeStruct(out.shape, out.dtype),
        [SMEM, SMEM] + [VMEM] * (len(parts) + 1) + [ANY],
        ANY,
        span * nocc * width * nao * tiles,
        span * width * nao * tiles,
        [pltpu.VMEM((span, width, nao), out.dtype), pltpu.SemaphoreType.DMA((span,))],
        {len(parts) + 3: 0},
    )(owner, table, *parts, occ_full, out)


def side_of(chips):
    side = math.isqrt(chips)
    while chips % side:
        side -= 1
    return side


def gather_rounds(aux):
    chips = aux // CORES
    nx = side_of(chips)
    ny = chips // nx

    def chip(y, x):
        return (y % ny) * nx + x % nx

    rounds = [(list(range(aux)), None, None)]
    index = {(0, 0): 0}
    order = [(a, 0) for a in range(1, nx)] + [(0, b) for b in range(1, ny)]
    order += [(a, b) for a in range(1, nx) for b in range(1, ny)]
    for a, b in order:
        source, pairs = [], []
        for d in range(aux):
            c, (y, x) = d % CORES, divmod(d // CORES, nx)
            turn = nx == ny and c == 1
            dx, dy = (b, a) if turn else (a, b)
            source.append(chip(y + dy, x + dx) * CORES + c)
            if a and b:
                dx, dy = (0, a) if turn else (a, 0)
            pairs.append((chip(y + dy, x + dx) * CORES + c, d))
        index[a, b] = len(rounds)
        rounds.append((source, pairs, index[0, b] if a and b else 0))
    return rounds


def per_device(density, occ_density, cabs_coeff, occ_coeff, tile_owner):
    local_q, nocc, depth = density.shape
    aux, owners = lax.axis_size("aux"), lax.axis_size("shell")
    rows = cabs_coeff.shape[0]
    nao = rows * aux
    ntile = tile_owner.shape[0]
    width = nao // ntile

    lanes = ((0, 0), (0, LANES - nocc))
    mine = jnp.concatenate([cabs_coeff, jnp.pad(occ_coeff, lanes)], axis=1)
    left = density.reshape(local_q * nocc, depth)
    occ = occ_density.reshape(local_q * nocc, nocc)
    owner = tile_owner.reshape(ntile)

    rounds = gather_rounds(aux)
    count = len(rounds)
    table = jnp.asarray([source for source, _, _ in rounds], jnp.int32)
    swap = [(d, d ^ 1) for d in range(aux)]
    hops = owners - 1
    half = (hops + 1) // 2
    arrived, pieces, partial, got = [], [], {}, {}

    def arrive(number):
        _, pairs, origin = rounds[number]
        value = mine
        if pairs is not None:
            value = arrived[origin]
            if number > 1:
                value = lax.optimization_barrier((value, arrived[-1]))[0]
            value = lax.ppermute(value, "aux", pairs)
        arrived.append(value)
        other = lax.ppermute(value, "aux", swap)
        pieces.append((value, other))
        partial[number] = matmul(left, occ, value, other)

    def terms(chunk):
        parts, near_of = [partial[chunk]], [None]
        for hop in range(hops):
            parts.append(got[chunk, hop])
            near_of.append(sorted({hop + 1, owners - 2 - hop}))
        return parts, near_of

    out = zero_slots(owner, (CAPT, local_q, width, nao), density.dtype)
    arrive(0)
    occ_full = None
    for step in range(count + hops):
        groups, values = [], []
        for hop in range(half):
            shared = [
                h for h in sorted({hop, hops - 1 - hop}) if 0 <= step - h < count
            ]
            if shared:
                groups.append(shared)
                values.append(
                    [
                        (partial[step - h],) + ((got[step - h, h - 1],) if h else ())
                        for h in shared
                    ]
                )
        new = {}
        if groups:
            if groups == [[0]]:
                sent = [values[0][0][0]]
            else:
                sent = send(owners, groups, values)
            for shared, value in zip(groups, sent):
                pairs = []
                for h in shared:
                    pairs += [(h, h + 1), (owners - 1 - h, owners - 2 - h)]
                result = lax.ppermute(value, "shell", pairs)
                for h in shared:
                    new[step - h, h] = result
        if step < count:
            first, second = pieces[step]
            occ_full = put_occ(table, step, first, second, nao, depth, occ_full)
        if step + 1 < count:
            arrive(step + 1)
        if step >= hops:
            chunk = step - hops
            parts, near_of = terms(chunk)
            out = final(owner, table, chunk, parts, near_of, occ_full, out, nocc)
        got.update(new)
    return out


def solution(mesh):
    in_specs = (
        P("aux", None, "shell"),
        P("aux", None, None),
        P("aux", "shell"),
        P("aux", None),
        P(),
    )
    out_specs = P("shell", "aux", None, None)

    return jax.shard_map(
        per_device, mesh=mesh, in_specs=in_specs, out_specs=out_specs, check_vma=False
    )
```

time: 177 us -> 128 us (0.72)
  blocking collectives: 62.4 us -> 0 us
  starting transfers between devices: 0.08 us -> 30.1 us
  Pallas kernels: 0 us -> 25.6 us
  matrix products: 19.3 us -> 0 us
  between operations: 13.2 us -> 0.45 us
  other arithmetic: 8.89 us -> 1.46 us
  waiting for transfers between devices: 71 us -> 68.6 us
    ppermute x0 -> x17, waiting for transfers between devices: none -> 68.6 us  [the longest x3 35 us: arrive(): value = lax.ppermute(value, 'aux', pairs)]
    all_gather x3 -> x0, blocking collectives: 62.4 us -> none  [the longest x2 51.6 us: per_device(): spread = lax.all_gather(rounded, 'shell', axis=1, tiled=True)]
    all_gather x1 -> x0, waiting for transfers between devices: 57.3 us -> none  [per_device(): lax.all_gather(cabs_coeff, 'aux', axis=0, tiled=True)]
    ppermute x0 -> x17, starting transfers between devices: none -> 30.1 us  [the longest x10 22.5 us: per_device(): result = lax.ppermute(value, 'shell', pairs)]
    pallas_call x0 -> x18, Pallas kernels: none -> 25.6 us  [the longest x4 16.1 us: final(): call(functools.partial(final_kernel, nocc, chunk, near_of), jax.ShapeDtyp...]
    dot_general x8 -> x0, matrix products: 19.3 us -> none  [the longest x2 13.5 us: per_device(): lax.dot_general(flat, lax.all_gather(cabs_coeff, 'aux', axis=0, tiled=Tru...]
    reduce_scatter x2 -> x0, waiting for transfers between devices: 12.9 us -> none  [per_device(): lax.psum_scatter(terms.astype(jnp.bfloat16), 'shell', scatter_dimension=1...]
    concatenate x1, other arithmetic: 6.71 us -> 1.46 us  [per_device(): mine = jnp.concatenate([cabs_coeff, jnp.pad(occ_coeff, lanes)], axis=1)]
  transfers between devices with their start and end apart: 3 -> 17, of which waited for: 3 -> 9; matrix products, arithmetic and copies ran while one was open for 6% -> 0% of each run, Pallas kernels for 0% -> 14%
where the time goes in v1:
time: 128 us; the launch traced here: 127 us
  waiting for transfers between devices  68.6 us (54%)
  starting transfers between devices  30.1 us (24%)
  Pallas kernels  25.6 us (20%)
  other arithmetic  1.46 us (1%)
    ppermute x3, waiting for transfers between devices, arrive(): value = lax.ppermute(value, 'aux', pairs)  35 us
    ppermute x10, waiting for transfers between devices, per_device(): result = lax.ppermute(value, 'shell', pairs)  33.6 us
    ppermute x10, starting transfers between devices, per_device(): result = lax.ppermute(value, 'shell', pairs)  22.5 us
    pallas_call x4, Pallas kernels, final(): call(functools.partial(final_kernel, nocc, chunk, near_of), jax.ShapeDtyp...  16.1 us
    ppermute x3, starting transfers between devices, arrive(): value = lax.ppermute(value, 'aux', pairs)  7.07 us
    pallas_call x4, Pallas kernels, matmul(): call(matmul_kernel, jax.ShapeDtypeStruct((rows, cols), left.dtype), [VMEM...  5.97 us
  transfers between devices with their start and end apart: 17, of which 9 were waited for; matrix products, arithmetic and copies ran while one was open for 0% of the time, Pallas kernels for 14%

profile of v1, /device:TPU:0, one launch (start us, length us, event | category | flops | bytes accessed | tf_op | source)
XLA Modules:
  0.0 127.2 jit_solution(4336937926035056448)
XLA Ops:
  0.0 0.9 copy.14
  1.0 1.5 %fusion.1.first_ref = bf16[256,2176]{1,0:T(8,128)(2,1)S(1)} fusion(bf16[256,120]{1,0:T(8,128)(2,1)S(1)} %copy.14, bf16[256,2048]{1,0:T(8,128)(2,1)} %param.8), kind=kLoop, calls=%fused_computation.2 | loop fusion | flops 3342336 | bytes 2224128 | tf_op jit(solution)/shard_map/concatenate | solution.py:266
  2.4 3.0 %collective-permute-start = (bf16[256,2176]{1,0:T(8,128)(2,1)S(1)}, bf16[256,2176]{1,0:T(8,128)(2,1)S(1)}, u32[]{:S(2)}, u32[]{:S(2)}) collective-permute-start(bf16[256,2176]{1,0:T(8,128)(2,1)S(1)} %fusion.1.first_ref), channel_id=1, source_target_pairs={{8,0},{20,4},{0,8},{28,12},{24,16},{4,20},{16,24},{12,28},{9,1},{2... | collective-permute-start | bytes 3342344 | tf_op jit(solution)/shard_map/ppermute | solution.py:286
  5.5 13.5 %collective-permute-done.first_ref = bf16[256,2176]{1,0:T(8,128)(2,1)S(1)} collective-permute-done((bf16[256,2176]{1,0:T(8,128)(2,1)S(1)}, bf16[256,2176]{1,0:T(8,128)(2,1)S(1)}, u32[]{:S(2)}, u32[]{:S(2)}) %collective-permute-start) | collective-permute-done | bytes 1114144 | tf_op jit(solution)/shard_map/ppermute | solution.py:286
  18.9 2.0 %collective-permute-start.1 = (bf16[256,2176]{1,0:T(8,128)(2,1)S(1)}, bf16[256,2176]{1,0:T(8,128)(2,1)S(1)}, u32[]{:S(2)}, u32[]{:S(2)}) collective-permute-start(bf16[256,2176]{1,0:T(8,128)(2,1)S(1)} %fusion.1.first_ref), channel_id=1, source_target_pairs={{16,0},{12,4},{24,8},{4,12},{0,16},{28,20},{8,24},{20,28},{17,1},{... | collective-permute-start | bytes 3342344 | tf_op jit(solution)/shard_map/ppermute | solution.py:286
  21.0 13.5 %collective-permute-done.1.first_ref = bf16[256,2176]{1,0:T(8,128)(2,1)S(1)} collective-permute-done((bf16[256,2176]{1,0:T(8,128)(2,1)S(1)}, bf16[256,2176]{1,0:T(8,128)(2,1)S(1)}, u32[]{:S(2)}, u32[]{:S(2)}) %collective-permute-start.1) | collective-permute-done | bytes 1114144 | tf_op jit(solution)/shard_map/ppermute | solution.py:286
  34.5 2.0 %collective-permute-start.2 = (bf16[256,2176]{1,0:T(8,128)(2,1)S(1)}, bf16[256,2176]{1,0:T(8,128)(2,1)S(1)}, u32[]{:S(2)}, u32[]{:S(2)}) collective-permute-start(bf16[256,2176]{1,0:T(8,128)(2,1)S(1)} %collective-permute-done.1.first_ref), channel_id=1, source_target_pairs={{8,0},{20,4},{0,8},{28,12},{24,16},{4,20},{16,24},{12,28},{9,1},{2... | collective-permute-start | bytes 3342344 | tf_op jit(solution)/shard_map/ppermute | solution.py:286
  37.0 1.5 %shard_map.67.refs_1_.refs_0_ = bf16[480,512]{1,0:T(8,128)(2,1)S(1)} custom-call(bf16[480,2048]{1,0:T(8,128)(2,1)S(1)} %bitcast.3, bf16[480,120]{1,0:T(8,128)(2,1)S(1)} %bitcast.7, bf16[256,2176]{1,0:T(8,128)(2,1)S(1)} %fusion.1.first_ref, bf16[256,2176]{1,0:T(8,128)(2,1)S(1)} %collective-permute-done.6.second_ref), custom_call_target="tpu_custom_call" | custom-call | flops 1006632960 | bytes 4063232 | tf_op jit(solution)/shard_map/pallas_call | solution.py:63
  38.5 3.4 %collective-permute-start.7 = (bf16[480,512]{1,0:T(8,128)(2,1)S(1)}, bf16[480,512]{1,0:T(8,128)(2,1)S(1)}, u32[]{:S(2)}, u32[]{:S(2)}) collective-permute-start(bf16[480,512]{1,0:T(8,128)(2,1)S(1)} %shard_map.67.refs_1_.refs_0_), channel_id=1, source_target_pairs={{0,1},{3,2},{4,5},{7,6},{8,9},{11,10},{12,13},{15,14},{16,17},{19,... | collective-permute-start | bytes 1474568 | tf_op jit(solution)/shard_map/ppermute | solution.py:326
  42.0 8.0 %collective-permute-done.2.first_ref = bf16[256,2176]{1,0:T(8,128)(2,1)S(1)} collective-permute-done((bf16[256,2176]{1,0:T(8,128)(2,1)S(1)}, bf16[256,2176]{1,0:T(8,128)(2,1)S(1)}, u32[]{:S(2)}, u32[]{:S(2)}) %collective-permute-start.2) | collective-permute-done | bytes 1114144 | tf_op jit(solution)/shard_map/ppermute | solution.py:286
  50.0 1.5 %shard_map.65.refs_0_.refs_3_.refs_1_ = bf16[480,512]{1,0:T(8,128)(2,1)S(1)} custom-call(bf16[480,2048]{1,0:T(8,128)(2,1)S(1)} %bitcast.4, bf16[480,120]{1,0:T(8,128)(2,1)S(1)} %bitcast.8, bf16[256,2176]{1,0:T(8,128)(2,1)S(1)} %collective-permute-done.first_ref, bf16[256,2176]{1,0:T(8,128)(2,1)S(1)} %collective-permute-done.4.second_ref), custom_call_target="tpu_custom_call" | custom-call | flops 1006632960 | bytes 4063232 | tf_op jit(solution)/shard_map/pallas_call | solution.py:63
  51.5 1.1 collective-permute-done.7.refs_2_.refs_1_
  52.6 0.7 collective-permute-start.8
  53.3 7.2 %collective-permute-start.9 = (bf16[480,512]{1,0:T(8,128)(2,1)S(1)}, bf16[480,512]{1,0:T(8,128)(2,1)S(1)}, u32[]{:S(2)}, u32[]{:S(2)}) collective-permute-start(bf16[480,512]{1,0:T(8,128)(2,1)S(1)} %get-tuple-element.18), channel_id=1, source_target_pairs={{0,1},{3,2},{4,5},{7,6},{8,9},{11,10},{12,13},{15,14},{16,17},{19,... | collective-permute-start | bytes 1474568 | tf_op jit(solution)/shard_map/ppermute | solution.py:326
  60.6 1.5 %shard_map.66.refs_0_.refs_3_ = bf16[480,512]{1,0:T(8,128)(2,1)S(1)} custom-call(bf16[480,2048]{1,0:T(8,128)(2,1)S(1)} %bitcast.5, bf16[480,120]{1,0:T(8,128)(2,1)S(1)} %bitcast.9, bf16[256,2176]{1,0:T(8,128)(2,1)S(1)} %collective-permute-done.1.first_ref, bf16[256,2176]{1,0:T(8,128)(2,1)S(1)} %collective-permute-done.5.second_ref), custom_call_target="tpu_custom_call" | custom-call | flops 1006632960 | bytes 4063232 | tf_op jit(solution)/shard_map/pallas_call | solution.py:63
  62.1 7.9 %collective-permute-done.9.refs_4_.refs_1_ = bf16[480,512]{1,0:T(8,128)(2,1)S(1)} collective-permute-done((bf16[480,512]{1,0:T(8,128)(2,1)S(1)}, bf16[480,512]{1,0:T(8,128)(2,1)S(1)}, u32[]{:S(2)}, u32[]{:S(2)}) %collective-permute-start.9) | collective-permute-done | bytes 491552 | tf_op jit(solution)/shard_map/ppermute | solution.py:326
  70.1 2.6 %collective-permute-start.11 = (bf16[480,512]{1,0:T(8,128)(2,1)S(1)}, bf16[480,512]{1,0:T(8,128)(2,1)S(1)}, u32[]{:S(2)}, u32[]{:S(2)}) collective-permute-start(bf16[480,512]{1,0:T(8,128)(2,1)S(1)} %get-tuple-element.20), channel_id=1, source_target_pairs={{0,1},{3,2},{2,3},{1,0},{4,5},{7,6},{6,7},{5,4},{8,9},{11,10},{10,... | collective-permute-start | bytes 1474568 | tf_op jit(solution)/shard_map/ppermute | solution.py:326
  72.7 0.7 collective-permute-start.10
  73.4 1.5 %shard_map.64.refs_0_.refs_2_ = bf16[480,512]{1,0:T(8,128)(2,1)S(1)} custom-call(bf16[480,2048]{1,0:T(8,128)(2,1)S(1)} %bitcast.6, bf16[480,120]{1,0:T(8,128)(2,1)S(1)} %bitcast.10, bf16[256,2176]{1,0:T(8,128)(2,1)S(1)} %collective-permute-done.2.first_ref, bf16[256,2176]{1,0:T(8,128)(2,1)S(1)} %collective-permute-done.3.second_ref), custom_call_target="tpu_custom_call" | custom-call | flops 1006632960 | bytes 4063232 | tf_op jit(solution)/shard_map/pallas_call | solution.py:63
  74.9 7.2 %collective-permute-done.11.refs_4_.refs_3_.refs_1_ = bf16[480,512]{1,0:T(8,128)(2,1)S(1)} collective-permute-done((bf16[480,512]{1,0:T(8,128)(2,1)S(1)}, bf16[480,512]{1,0:T(8,128)(2,1)S(1)}, u32[]{:S(2)}, u32[]{:S(2)}) %collective-permute-start.11) | collective-permute-done | bytes 491552 | tf_op jit(solution)/shard_map/ppermute | solution.py:326
  82.1 3.8 %collective-permute-start.12 = (bf16[480,512]{1,0:T(8,128)(2,1)S(1)}, bf16[480,512]{1,0:T(8,128)(2,1)S(1)}, u32[]{:S(2)}, u32[]{:S(2)}) collective-permute-start(bf16[480,512]{1,0:T(8,128)(2,1)S(1)} %get-tuple-element.21), channel_id=1, source_target_pairs={{0,1},{3,2},{2,3},{1,0},{4,5},{7,6},{6,7},{5,4},{8,9},{11,10},{10,... | collective-permute-start | bytes 1474568 | tf_op jit(solution)/shard_map/ppermute | solution.py:326
  86.6 7.9 %collective-permute-done.12.refs_3_.refs_1_ = bf16[480,512]{1,0:T(8,128)(2,1)S(1)} collective-permute-done((bf16[480,512]{1,0:T(8,128)(2,1)S(1)}, bf16[480,512]{1,0:T(8,128)(2,1)S(1)}, u32[]{:S(2)}, u32[]{:S(2)}) %collective-permute-start.12) | collective-permute-done | bytes 491552 | tf_op jit(solution)/shard_map/ppermute | solution.py:326
  94.5 0.8 collective-permute-start.14
  95.3 1.3 %collective-permute-start.16 = (bf16[480,512]{1,0:T(8,128)(2,1)S(1)}, bf16[480,512]{1,0:T(8,128)(2,1)S(1)}, u32[]{:S(2)}, u32[]{:S(2)}) collective-permute-start(bf16[480,512]{1,0:T(8,128)(2,1)S(1)} %get-tuple-element.24), channel_id=1, source_target_pairs={{2,3},{1,0},{6,7},{5,4},{10,11},{9,8},{14,15},{13,12},{18,19},{17,... | collective-permute-start | bytes 1474568 | tf_op jit(solution)/shard_map/ppermute | solution.py:326
  96.6 1.3 %collective-permute-start.15 = (bf16[480,512]{1,0:T(8,128)(2,1)S(1)}, bf16[480,512]{1,0:T(8,128)(2,1)S(1)}, u32[]{:S(2)}, u32[]{:S(2)}) collective-permute-start(bf16[480,512]{1,0:T(8,128)(2,1)S(1)} %shard_map.72), channel_id=1, source_target_pairs={{2,3},{1,0},{6,7},{5,4},{10,11},{9,8},{14,15},{13,12},{18,19},{17,... | collective-permute-start | bytes 1474568 | tf_op jit(solution)/shard_map/ppermute | solution.py:326
  97.9 0.9 shard_map.77.refs_5_
  101.4 2.5 %shard_map.78.refs_5_ = bf16[8,4,128,2048]{3,2,1,0:T(8,128)(2,1)} custom-call(s32[16]{0:T(128)S(1)} %bitcast.12, s32[4,8]{1,0:T(4,128)S(1)} %copy-done.2, bf16[480,512]{1,0:T(8,128)(2,1)S(1)} %shard_map.67.refs_1_.refs_0_, bf16[480,512]{1,0:T(8,128)(2,1)S(1)} %collective-permute-done.7.refs_2_.refs_1_, ...), custom_call_target="tpu_custom_call", output_to_operand_aliasing={{}: (7, {})} | custom-call | flops 503316480 | bytes 4194304 | tf_op jit(solution)/shard_map/pallas_call | solution.py:211
  103.9 0.8 shard_map.79.refs_5_
  104.7 6.6 %collective-permute-done.16.refs_3_ = bf16[480,512]{1,0:T(8,128)(2,1)S(1)} collective-permute-done((bf16[480,512]{1,0:T(8,128)(2,1)S(1)}, bf16[480,512]{1,0:T(8,128)(2,1)S(1)}, u32[]{:S(2)}, u32[]{:S(2)}) %collective-permute-start.16) | collective-permute-done | bytes 491552 | tf_op jit(solution)/shard_map/ppermute | solution.py:326
  111.3 5.6 %shard_map.80.refs_5_ = bf16[8,4,128,2048]{3,2,1,0:T(8,128)(2,1)} custom-call(s32[16]{0:T(128)S(1)} %bitcast.14, s32[4,8]{1,0:T(4,128)S(1)} %copy-done.2, bf16[480,512]{1,0:T(8,128)(2,1)S(1)} %shard_map.66.refs_0_.refs_3_, bf16[480,512]{1,0:T(8,128)(2,1)S(1)} %collective-permute-done.11.refs_4_.refs_3_.refs_1_, ...), custom_call_target="tpu_custom_call", output_to_operand_aliasing={{}: (7, {})} | custom-call | flops 503316480 | bytes 4194304 | tf_op jit(solution)/shard_map/pallas_call | solution.py:211
  116.9 2.9 %collective-permute-done.15.refs_3_ = bf16[480,512]{1,0:T(8,128)(2,1)S(1)} collective-permute-done((bf16[480,512]{1,0:T(8,128)(2,1)S(1)}, bf16[480,512]{1,0:T(8,128)(2,1)S(1)}, u32[]{:S(2)}, u32[]{:S(2)}) %collective-permute-start.15) | collective-permute-done | bytes 491552 | tf_op jit(solution)/shard_map/ppermute | solution.py:326
  119.8 7.2 %shard_map.81 = bf16[8,4,128,2048]{3,2,1,0:T(8,128)(2,1)} custom-call(s32[16]{0:T(128)S(1)} %bitcast.15, s32[4,8]{1,0:T(4,128)S(1)} %copy-done.2, bf16[480,512]{1,0:T(8,128)(2,1)S(1)} %shard_map.64.refs_0_.refs_2_, bf16[480,512]{1,0:T(8,128)(2,1)S(1)} %collective-permute-done.12.refs_3_.refs_1_, ...), custom_call_target="tpu_custom_call", output_to_operand_aliasing={{}: (7, {})} | custom-call | flops 503316480 | bytes 4194304 | tf_op jit(solution)/shard_map/pallas_call | solution.py:211
  (30 shorter events, 3.9 us)
Async XLA Ops:
  0.9 36.0 %copy-start = (bf16[4,120,2048]{2,1,0:T(8,128)(2,1)S(1)}, bf16[4,120,2048]{2,1,0:T(8,128)(2,1)}, u32[]{:S(2)}) copy-start(bf16[4,120,2048]{2,1,0:T(8,128)(2,1)} %param.6) | copy-start | bytes 5898244
  1.0 36.0 %copy-start.1 = (bf16[4,120,120]{2,1,0:T(8,128)(2,1)S(1)}, bf16[4,120,120]{2,1,0:T(8,128)(2,1)}, u32[]{:S(2)}) copy-start(bf16[4,120,120]{2,1,0:T(8,128)(2,1)} %param.7) | copy-start | bytes 345604
  2.4 16.5 %collective-permute-start = (bf16[256,2176]{1,0:T(8,128)(2,1)S(1)}, bf16[256,2176]{1,0:T(8,128)(2,1)S(1)}, u32[]{:S(2)}, u32[]{:S(2)}) collective-permute-start(bf16[256,2176]{1,0:T(8,128)(2,1)S(1)} %fusion.1.first_ref), channel_id=1, source_target_pairs={{8,0},{20,4},{0,8},{28,12},{24,16},{4,20},{16,24},{12,28},{9,1},{2... | collective-permute-start | bytes 3342344 | tf_op jit(solution)/shard_map/ppermute | solution.py:286
  18.9 15.5 %collective-permute-start.1 = (bf16[256,2176]{1,0:T(8,128)(2,1)S(1)}, bf16[256,2176]{1,0:T(8,128)(2,1)S(1)}, u32[]{:S(2)}, u32[]{:S(2)}) collective-permute-start(bf16[256,2176]{1,0:T(8,128)(2,1)S(1)} %fusion.1.first_ref), channel_id=1, source_target_pairs={{16,0},{12,4},{24,8},{4,12},{0,16},{28,20},{8,24},{20,28},{17,1},{... | collective-permute-start | bytes 3342344 | tf_op jit(solution)/shard_map/ppermute | solution.py:286
  21.0 16.0 %collective-permute-start.6 = (bf16[256,2176]{1,0:T(8,128)(2,1)S(1)}, bf16[256,2176]{1,0:T(8,128)(2,1)S(1)}, u32[]{:S(2)}, u32[]{:S(2)}) collective-permute-start(bf16[256,2176]{1,0:T(8,128)(2,1)S(1)} %fusion.1.first_ref), channel_id=1, source_target_pairs={{0,4},{4,0},{8,12},{12,8},{16,20},{20,16},{24,28},{28,24},{1,5},{5... | collective-permute-start | bytes 3342344 | tf_op jit(solution)/shard_map/ppermute | solution.py:288
  34.5 15.5 %collective-permute-start.2 = (bf16[256,2176]{1,0:T(8,128)(2,1)S(1)}, bf16[256,2176]{1,0:T(8,128)(2,1)S(1)}, u32[]{:S(2)}, u32[]{:S(2)}) collective-permute-start(bf16[256,2176]{1,0:T(8,128)(2,1)S(1)} %collective-permute-done.1.first_ref), channel_id=1, source_target_pairs={{8,0},{20,4},{0,8},{28,12},{24,16},{4,20},{16,24},{12,28},{9,1},{2... | collective-permute-start | bytes 3342344 | tf_op jit(solution)/shard_map/ppermute | solution.py:286
  36.5 13.5 %collective-permute-start.4 = (bf16[256,2176]{1,0:T(8,128)(2,1)S(1)}, bf16[256,2176]{1,0:T(8,128)(2,1)S(1)}, u32[]{:S(2)}, u32[]{:S(2)}) collective-permute-start(bf16[256,2176]{1,0:T(8,128)(2,1)S(1)} %collective-permute-done.first_ref), channel_id=1, source_target_pairs={{0,4},{4,0},{8,12},{12,8},{16,20},{20,16},{24,28},{28,24},{1,5},{5... | collective-permute-start | bytes 3342344 | tf_op jit(solution)/shard_map/ppermute | solution.py:288
  36.5 24.1 %collective-permute-start.5 = (bf16[256,2176]{1,0:T(8,128)(2,1)S(1)}, bf16[256,2176]{1,0:T(8,128)(2,1)S(1)}, u32[]{:S(2)}, u32[]{:S(2)}) collective-permute-start(bf16[256,2176]{1,0:T(8,128)(2,1)S(1)} %collective-permute-done.1.first_ref), channel_id=1, source_target_pairs={{0,4},{4,0},{8,12},{12,8},{16,20},{20,16},{24,28},{28,24},{1,5},{5... | collective-permute-start | bytes 3342344 | tf_op jit(solution)/shard_map/ppermute | solution.py:288
  38.5 14.1 %collective-permute-start.7 = (bf16[480,512]{1,0:T(8,128)(2,1)S(1)}, bf16[480,512]{1,0:T(8,128)(2,1)S(1)}, u32[]{:S(2)}, u32[]{:S(2)}) collective-permute-start(bf16[480,512]{1,0:T(8,128)(2,1)S(1)} %shard_map.67.refs_1_.refs_0_), channel_id=1, source_target_pairs={{0,1},{3,2},{4,5},{7,6},{8,9},{11,10},{12,13},{15,14},{16,17},{19,... | collective-permute-start | bytes 1474568 | tf_op jit(solution)/shard_map/ppermute | solution.py:326
  50.0 23.4 %collective-permute-start.3 = (bf16[256,2176]{1,0:T(8,128)(2,1)S(1)}, bf16[256,2176]{1,0:T(8,128)(2,1)S(1)}, u32[]{:S(2)}, u32[]{:S(2)}) collective-permute-start(bf16[256,2176]{1,0:T(8,128)(2,1)S(1)} %collective-permute-done.2.first_ref), channel_id=1, source_target_pairs={{0,4},{4,0},{8,12},{12,8},{16,20},{20,16},{24,28},{28,24},{1,5},{5... | collective-permute-start | bytes 3342344 | tf_op jit(solution)/shard_map/ppermute | solution.py:288
  52.6 9.5 %collective-permute-start.8 = (bf16[480,512]{1,0:T(8,128)(2,1)S(1)}, bf16[480,512]{1,0:T(8,128)(2,1)S(1)}, u32[]{:S(2)}, u32[]{:S(2)}) collective-permute-start(bf16[480,512]{1,0:T(8,128)(2,1)S(1)} %get-tuple-element.17), channel_id=1, source_target_pairs={{1,2},{2,1},{5,6},{6,5},{9,10},{10,9},{13,14},{14,13},{17,18},{18,... | collective-permute-start | bytes 1474568 | tf_op jit(solution)/shard_map/ppermute | solution.py:326
  53.3 16.7 %collective-permute-start.9 = (bf16[480,512]{1,0:T(8,128)(2,1)S(1)}, bf16[480,512]{1,0:T(8,128)(2,1)S(1)}, u32[]{:S(2)}, u32[]{:S(2)}) collective-permute-start(bf16[480,512]{1,0:T(8,128)(2,1)S(1)} %get-tuple-element.18), channel_id=1, source_target_pairs={{0,1},{3,2},{4,5},{7,6},{8,9},{11,10},{12,13},{15,14},{16,17},{19,... | collective-permute-start | bytes 1474568 | tf_op jit(solution)/shard_map/ppermute | solution.py:326
  70.1 12.0 %collective-permute-start.11 = (bf16[480,512]{1,0:T(8,128)(2,1)S(1)}, bf16[480,512]{1,0:T(8,128)(2,1)S(1)}, u32[]{:S(2)}, u32[]{:S(2)}) collective-permute-start(bf16[480,512]{1,0:T(8,128)(2,1)S(1)} %get-tuple-element.20), channel_id=1, source_target_pairs={{0,1},{3,2},{2,3},{1,0},{4,5},{7,6},{6,7},{5,4},{8,9},{11,10},{10,... | collective-permute-start | bytes 1474568 | tf_op jit(solution)/shard_map/ppermute | solution.py:326
  72.7 9.4 %collective-permute-start.10 = (bf16[480,512]{1,0:T(8,128)(2,1)S(1)}, bf16[480,512]{1,0:T(8,128)(2,1)S(1)}, u32[]{:S(2)}, u32[]{:S(2)}) collective-permute-start(bf16[480,512]{1,0:T(8,128)(2,1)S(1)} %get-tuple-element.19), channel_id=1, source_target_pairs={{1,2},{2,1},{5,6},{6,5},{9,10},{10,9},{13,14},{14,13},{17,18},{18,... | collective-permute-start | bytes 1474568 | tf_op jit(solution)/shard_map/ppermute | solution.py:326
  82.1 12.3 %collective-permute-start.12 = (bf16[480,512]{1,0:T(8,128)(2,1)S(1)}, bf16[480,512]{1,0:T(8,128)(2,1)S(1)}, u32[]{:S(2)}, u32[]{:S(2)}) collective-permute-start(bf16[480,512]{1,0:T(8,128)(2,1)S(1)} %get-tuple-element.21), channel_id=1, source_target_pairs={{0,1},{3,2},{2,3},{1,0},{4,5},{7,6},{6,7},{5,4},{8,9},{11,10},{10,... | collective-permute-start | bytes 1474568 | tf_op jit(solution)/shard_map/ppermute | solution.py:326
  85.9 8.6 %collective-permute-start.13 = (bf16[480,512]{1,0:T(8,128)(2,1)S(1)}, bf16[480,512]{1,0:T(8,128)(2,1)S(1)}, u32[]{:S(2)}, u32[]{:S(2)}) collective-permute-start(bf16[480,512]{1,0:T(8,128)(2,1)S(1)} %get-tuple-element.22), channel_id=1, source_target_pairs={{1,2},{2,1},{5,6},{6,5},{9,10},{10,9},{13,14},{14,13},{17,18},{18,... | collective-permute-start | bytes 1474568 | tf_op jit(solution)/shard_map/ppermute | solution.py:326
  94.5 3.5 %copy-start.3 = (s32[16,1]{0,1:T(1,128)S(1)}, s32[16,1]{0,1:T(1,128)}, u32[]{:S(2)}) copy-start(s32[16,1]{0,1:T(1,128)} %param.10) | copy-start | bytes 196
  94.5 2.1 %collective-permute-start.14 = (bf16[480,512]{1,0:T(8,128)(2,1)S(1)}, bf16[480,512]{1,0:T(8,128)(2,1)S(1)}, u32[]{:S(2)}, u32[]{:S(2)}) collective-permute-start(bf16[480,512]{1,0:T(8,128)(2,1)S(1)} %get-tuple-element.23), channel_id=1, source_target_pairs={{1,2},{2,1},{5,6},{6,5},{9,10},{10,9},{13,14},{14,13},{17,18},{18,... | collective-permute-start | bytes 1474568 | tf_op jit(solution)/shard_map/ppermute | solution.py:326
  95.3 16.0 %collective-permute-start.16 = (bf16[480,512]{1,0:T(8,128)(2,1)S(1)}, bf16[480,512]{1,0:T(8,128)(2,1)S(1)}, u32[]{:S(2)}, u32[]{:S(2)}) collective-permute-start(bf16[480,512]{1,0:T(8,128)(2,1)S(1)} %get-tuple-element.24), channel_id=1, source_target_pairs={{2,3},{1,0},{6,7},{5,4},{10,11},{9,8},{14,15},{13,12},{18,19},{17,... | collective-permute-start | bytes 1474568 | tf_op jit(solution)/shard_map/ppermute | solution.py:326
  96.6 23.2 %collective-permute-start.15 = (bf16[480,512]{1,0:T(8,128)(2,1)S(1)}, bf16[480,512]{1,0:T(8,128)(2,1)S(1)}, u32[]{:S(2)}, u32[]{:S(2)}) collective-permute-start(bf16[480,512]{1,0:T(8,128)(2,1)S(1)} %shard_map.72), channel_id=1, source_target_pairs={{2,3},{1,0},{6,7},{5,4},{10,11},{9,8},{14,15},{13,12},{18,19},{17,... | collective-permute-start | bytes 1474568 | tf_op jit(solution)/shard_map/ppermute | solution.py:326
  97.9 0.9 copy-start.2
